TPU v7x, 256 devices: a whole 4x4x8 slice. The times are simulated.
256 devices in a mesh: tm: 8 (over z), row: 4 (over y), col: 8 (over x, core).
Axes of the slice: x: 4, y: 4, z: 8, core: 2. Of those that a mesh axis runs over, the one named last changes fastest.
Arguments:
- latent: bfloat16 [32, 64, 192, 256], P('tm', 'row', 'col'), may hold values from -43 to 43
- gain_first: float32 [256], replicated, may hold values from 0.5 to 1.5
- bias_first: float32 [256], replicated, may hold values from -3 to 3
- kernel_first: bfloat16 [3, 3, 3, 256, 256], replicated, may hold values from -0.078125 to 0.078125
- gain_second: float32 [256], replicated, may hold values from 0.5 to 1.5
- bias_second: float32 [256], replicated, may hold values from -3 to 3
- kernel_second: bfloat16 [3, 3, 3, 256, 256], replicated, may hold values from -0.078125 to 0.078125
- conv_bias: float32 [256], replicated, may hold values from -3 to 3
Outputs:
- upsampled: bfloat16 [32, 128, 384, 256], P('tm', 'row', 'col')
All inputs are finite; a program needn't handle non-finite values.
Results may differ from a plain program's by a relative error of at most 0.006.
Values may be sent and summed in bfloat16 or wider, within the bound.
A program may use at most 64 MiB of HBM per device.

v0:
```python
import jax
import jax.numpy as jnp
from jax import lax
from jax.sharding import PartitionSpec as P

C = 256
GROUPS = 32


EPSILON = 1e-06


def entering(x, axis, combine, identity):
    peers, here = (lax.axis_size(axis), lax.axis_index(axis))
    everything = jax.tree.map(lambda part: lax.all_gather(part, axis), x)
    start = jax.tree.map(
        lambda part, zero: jnp.broadcast_to(jnp.asarray(zero, part.dtype), part.shape), x, identity
    )

    def hop(k, before):
        reached = k < here
        new = combine(before, jax.tree.map(lambda part: part[k], everything))
        return jax.tree.map(lambda a, b: jnp.where(reached, a, b), new, before)

    return lax.fori_loop(0, peers, hop, start)


def from_behind(block, axis, distance):
    devices = range(lax.axis_size(axis))
    route = [(i - distance, i) for i in devices if i - distance in devices]
    return lax.ppermute(block, axis, route)


def extended(x, sides, width):
    for axis, dim in sides:
        peers, length = (lax.axis_size(axis), x.shape[dim])
        up = [(i, (i + 1) % peers) for i in range(peers - 1)]
        down = [(j, i) for i, j in up]
        last = lax.slice_in_dim(x, length - width, length, axis=dim)
        leading = lax.slice_in_dim(x, 0, width, axis=dim)
        before = lax.ppermute(last, axis, up)
        after = lax.ppermute(leading, axis, down)
        x = jnp.concatenate([before, x, after], axis=dim)
    return x


def channel_terms(group_sum, group_square, cell_count):
    group_mean = group_sum / cell_count
    norm_scale = lax.rsqrt(group_square / cell_count - group_mean * group_mean + EPSILON)
    return (jnp.repeat(group_mean, C // GROUPS), jnp.repeat(norm_scale, C // GROUPS))


def add_pair(leading, trailing):
    return (leading[0] + trailing[0], leading[1] + trailing[1])


def span_moments(source):
    values = source.astype(jnp.float32)
    grouped = values.reshape(-1, GROUPS, C // GROUPS)
    local_sum = jnp.sum(grouped, axis=(0, 2))
    local_square = jnp.sum(grouped * grouped, axis=(0, 2))
    span_index = lax.axis_index("tm")
    tile_sum, tile_square = lax.psum((local_sum, local_square), ("row", "col"))
    empty_vec = jnp.zeros_like(tile_sum)
    prior_sum, prior_square = entering(
        (tile_sum, tile_square), "tm", add_pair, (empty_vec, empty_vec)
    )
    upto_sum = prior_sum + tile_sum
    upto_square = prior_square + tile_square
    per_span = (
        source.shape[0]
        * source.shape[1]
        * lax.axis_size("row")
        * source.shape[2]
        * lax.axis_size("col")
        * (C // GROUPS)
    )
    span_done = span_index.astype(jnp.float32)
    prior_terms = channel_terms(prior_sum, prior_square, jnp.maximum(span_done, 1.0) * per_span)
    upto_terms = channel_terms(upto_sum, upto_square, (span_done + 1.0) * per_span)
    return (prior_terms, upto_terms)


def widen_block(own_block):
    frame_cache = from_behind(own_block[-2:], "tm", 1)
    longer = jnp.concatenate([frame_cache, own_block], 0)
    return extended(longer, (("row", 1), ("col", 2)), 1)


def norm_conv_input(source, norm_gain, norm_bias):
    prior_terms, upto_terms = span_moments(source)
    values = source.astype(jnp.float32)
    activated = jax.nn.silu(
        (values - upto_terms[0]) * (upto_terms[1] * norm_gain) + norm_bias
    ).astype(jnp.bfloat16)
    return widen_block(activated)


def conv_block(padded, kernel):
    span_frames = padded.shape[0] - 2
    tile_rows = padded.shape[1] - 2
    tile_cols = padded.shape[2] - 2
    channels = padded.shape[3]
    running = jnp.zeros((span_frames * tile_rows * tile_cols, kernel.shape[-1]), jnp.float32)
    for tap_row in range(3):
        for tap_col in range(3):
            window = padded[:, tap_row : tap_row + tile_rows, tap_col : tap_col + tile_cols, :]
            stacked = jnp.concatenate(
                [window[tap_time : tap_time + span_frames] for tap_time in range(3)], axis=3
            )
            running = running + jnp.dot(
                stacked.reshape(-1, 3 * channels),
                kernel[:, tap_row, tap_col].reshape(3 * channels, -1),
                preferred_element_type=jnp.float32,
            )
    return running.reshape(span_frames, tile_rows, tile_cols, -1)


def on_device(
    latent, gain_first, bias_first, kernel_first, gain_second, bias_second, kernel_second, conv_bias
):
    hidden = conv_block(norm_conv_input(latent, gain_first, bias_first), kernel_first).astype(
        jnp.bfloat16
    )
    branch = conv_block(norm_conv_input(hidden, gain_second, bias_second), kernel_second)
    summed = (latent.astype(jnp.float32) + branch + conv_bias).astype(jnp.bfloat16)
    return jnp.repeat(jnp.repeat(summed, 2, axis=1), 2, axis=2)


def solution(mesh):
    return jax.shard_map(
        on_device,
        mesh=mesh,
        in_specs=(P("tm", "row", "col", None), P(), P(), P(), P(), P(), P(), P()),
        out_specs=P("tm", "row", "col", None),
        check_vma=False,
    )
```

profile of v0, /device:TPU:1, one launch (start us, length us, event | category | flops | bytes accessed | tf_op | source)
XLA Modules:
  0.0 260.1 jit_solution(14331374951814830136)
XLA Ops:
  0.0 1.4 fusion.6
  1.8 65.3 %all-reduce.5 = (f32[32]{0:T(128)S(1)}, f32[32]{0:T(128)S(1)}) all-reduce(f32[32]{0:T(128)S(1)} %reduce_sum.51, f32[32]{0:T(128)S(1)} %reduce_sum.54), channel_id=1, replica_groups=mesh['tm'=8,'row'=4,'col'=8] {'row','col'}, use_global_device_ids=true, to_apply=%region_2.0 | all-reduce | flops 64 | bytes 512 | tf_op jit(solution)/shard_map/psum | solution.py:63
  67.1 1.3 dynamic-slice
  69.5 14.8 %all-reduce.7 = (f32[256]{0:T(256)S(1)}, f32[256]{0:T(256)S(1)}) all-reduce(f32[256]{0:T(256)S(1)} %dynamic-update-slice, f32[256]{0:T(256)S(1)} %dynamic-update-slice.1), channel_id=2, replica_groups=mesh['tm'=8,'row'=4,'col'=8] {'tm'}, use_global_device_ids=true, to_apply=%add | all-reduce | flops 512 | bytes 4096
  85.7 1.6 fusion.14
  87.4 1.4 collective-permute-start
  88.9 2.3 fusion.20
  91.2 2.4 collective-permute-done
  93.6 1.3 collective-permute-start.2
  94.9 4.0 %collective-permute-start.1 = (bf16[6,1,24,256]{3,2,1,0:T(8,128)(2,1)S(1)}, bf16[6,1,24,256]{3,2,1,0:T(8,128)(2,1)S(1)}, u32[]{:S(2)}, u32[]{:S(2)}) collective-permute-start(bf16[6,1,24,256]{3,2,1,0:T(8,128)(2,1)S(1)} %get-tuple-element.395), channel_id=1, source_target_pairs={{0,8},{8,16},{16,24},{1,9},{9,17},{17,25},{2,10},{10,18},{18,26},{... | collective-permute-start | bytes 221192 | tf_op jit(solution)/shard_map/ppermute | solution.py:41
  99.1 1.1 collective-permute-done.1
  100.5 12.6 %collective-permute-start.4 = (bf16[6,18,1,256]{3,2,1,0:T(2,128)(2,1)S(1)}, bf16[6,18,1,256]{3,2,1,0:T(2,128)(2,1)S(1)}, u32[]{:S(2)}, u32[]{:S(2)}) collective-permute-start(bf16[6,18,1,256]{3,2,1,0:T(2,128)(2,1)S(1)} %get-tuple-element.375), channel_id=1, source_target_pairs={{1,0},{2,1},{3,2},{4,3},{5,4},{6,5},{7,6},{9,8},{10,9},{11,10},{12... | collective-permute-start | bytes 165896 | tf_op jit(solution)/shard_map/ppermute | solution.py:42
  113.1 2.1 collective-permute-start.3
  116.8 1.2 pad_maximum_fusion.18
  118.6 5.1 %fusion.23 = (bf16[4,16,24,256]{3,2,1,0:T(8,128)(2,1)S(1)}, bf16[4,16,24,256]{3,2,1,0:T(8,128)(2,1)S(1)}, bf16[4,16,24,256]{3,2,1,0:T(8,128)(2,1)S(1)}, bf16[4,1...) fusion(bf16[6,18,25,256]{3,2,1,0:T(8,128)(2,1)S(1)} %get-tuple-, ...), kind=kLoop, calls=%fused_computation.101 | loop fusion | bytes 14155776 | tf_op jit(solution)/shard_map/slice | solution.py:109
  124.1 0.8 fusion.29
  124.9 0.8 convolution_add_fusion.15
  126.0 0.8 convolution_add_fusion.14
  126.8 0.8 convolution_add_fusion.13
  127.6 0.8 convolution_add_fusion.12
  128.4 0.8 convolution_add_fusion.11
  129.3 0.8 convolution_add_fusion.10
  130.1 0.8 convolution_add_fusion.9
  131.1 0.8 multiply_reduce_fusion
  132.3 62.2 %all-reduce.4 = (f32[32]{0:T(128)S(1)}, f32[32]{0:T(128)S(1)}) all-reduce(f32[32]{0:T(128)S(1)} %reduce_sum.72, f32[32]{0:T(128)S(1)} %reduce_sum.75), channel_id=1, replica_groups=mesh['tm'=8,'row'=4,'col'=8] {'row','col'}, use_global_device_ids=true, to_apply=%region_10.11 | all-reduce | flops 64 | bytes 512 | tf_op jit(solution)/shard_map/psum | solution.py:63
  194.9 13.0 %all-reduce.6 = (f32[256]{0:T(256)S(1)}, f32[256]{0:T(256)S(1)}) all-reduce(f32[256]{0:T(256)S(1)} %dynamic-update-slice.2, f32[256]{0:T(256)S(1)} %dynamic-update-slice.3), channel_id=4, replica_groups=mesh['tm'=8,'row'=4,'col'=8] {'tm'}, use_global_device_ids=true, to_apply=%add.2 | all-reduce | flops 512 | bytes 4096
  209.2 2.5 collective-permute-start.5
  211.8 2.3 fusion.19
  214.1 2.3 collective-permute-done.5
  216.5 1.3 collective-permute-start.7
  217.8 4.0 %collective-permute-start.6 = (bf16[6,1,24,256]{3,2,1,0:T(8,128)(2,1)S(1)}, bf16[6,1,24,256]{3,2,1,0:T(8,128)(2,1)S(1)}, u32[]{:S(2)}, u32[]{:S(2)}) collective-permute-start(bf16[6,1,24,256]{3,2,1,0:T(8,128)(2,1)S(1)} %get-tuple-element.391), channel_id=1, source_target_pairs={{0,8},{8,16},{16,24},{1,9},{9,17},{17,25},{2,10},{10,18},{18,26},{... | collective-permute-start | bytes 221192 | tf_op jit(solution)/shard_map/ppermute | solution.py:41
  222.0 1.1 collective-permute-done.6
  223.3 8.9 %collective-permute-start.9 = (bf16[6,18,1,256]{3,2,1,0:T(2,128)(2,1)S(1)}, bf16[6,18,1,256]{3,2,1,0:T(2,128)(2,1)S(1)}, u32[]{:S(2)}, u32[]{:S(2)}) collective-permute-start(bf16[6,18,1,256]{3,2,1,0:T(2,128)(2,1)S(1)} %get-tuple-element.371), channel_id=1, source_target_pairs={{1,0},{2,1},{3,2},{4,3},{5,4},{6,5},{7,6},{9,8},{10,9},{11,10},{12... | collective-permute-start | bytes 165896 | tf_op jit(solution)/shard_map/ppermute | solution.py:42
  232.2 1.9 collective-permute-start.8
  235.9 1.2 pad_maximum_fusion.19
  237.7 5.4 %fusion.21 = (bf16[4,16,24,256]{3,2,1,0:T(8,128)(2,1)S(1)}, bf16[4,16,24,256]{3,2,1,0:T(8,128)(2,1)S(1)}, bf16[4,16,24,256]{3,2,1,0:T(8,128)(2,1)S(1)}, bf16[4,1...) fusion(bf16[6,18,25,256]{3,2,1,0:T(8,128)(2,1)S(1)} %get-tuple-, ...), kind=kLoop, calls=%fused_computation.99 | loop fusion | bytes 14155776 | tf_op jit(solution)/shard_map/slice | solution.py:109
  243.3 0.8 fusion.30
  244.1 0.8 convolution_add_fusion.7
  245.0 0.8 convolution_add_fusion.6
  246.0 0.8 convolution_add_fusion.5
  246.7 0.8 convolution_add_fusion.4
  247.7 0.8 convolution_add_fusion.3
  248.6 0.8 convolution_add_fusion.2
  249.4 0.8 convolution_add_fusion.1
  250.4 0.8 convolution_add_fusion
  251.8 1.2 broadcast_in_dim.27
  253.0 3.9 %broadcast_in_dim.28 = bf16[4,32,24,2,256]{4,3,2,1,0:T(2,128)(2,1)S(1)} broadcast(bf16[4,32,24,256]{3,2,1,0:T(8,128)(2,1)} %bitcast.108), dimensions={0,1,2,4} | broadcast | bytes 4718592 | tf_op jit(solution)/shard_map/broadcast_in_dim | solution.py:127
  256.9 3.2 %reshape.109 = bf16[4,32,48,256]{3,2,1,0:T(8,128)(2,1)} reshape(bf16[4,32,24,2,256]{4,3,2,1,0:T(2,128)(2,1)S(1)} %broadcast_in_dim.28) | data formatting | bytes 6291456 | tf_op jit(solution)/shard_map/reshape | solution.py:127
  (101 shorter events, 12.4 us)
Async XLA Ops:
  87.4 6.2 %collective-permute-start = (bf16[2,16,24,256]{3,2,1,0:T(8,128)(2,1)S(1)}, bf16[2,16,24,256]{3,2,1,0:T(8,128)(2,1)S(1)}, u32[]{:S(2)}, u32[]{:S(2)}) collective-permute-start(bf16[2,16,24,256]{3,2,1,0:T(8,128)(2,1)S(1)} %slice.400), channel_id=1, source_target_pairs={{0,32},{32,64},{64,96},{96,128},{128,160},{160,192},{192,224},{1,3... | collective-permute-start | bytes 1179656 | tf_op jit(solution)/shard_map/ppermute | solution.py:31
  93.6 5.5 %collective-permute-start.2 = (bf16[6,1,24,256]{3,2,1,0:T(8,128)(2,1)S(1)}, bf16[6,1,24,256]{3,2,1,0:T(8,128)(2,1)S(1)}, u32[]{:S(2)}, u32[]{:S(2)}) collective-permute-start(bf16[6,1,24,256]{3,2,1,0:T(8,128)(2,1)S(1)} %get-tuple-element.396), channel_id=1, source_target_pairs={{8,0},{16,8},{24,16},{9,1},{17,9},{25,17},{10,2},{18,10},{26,18},{... | collective-permute-start | bytes 221192 | tf_op jit(solution)/shard_map/ppermute | solution.py:42
  94.9 5.4 %collective-permute-start.1 = (bf16[6,1,24,256]{3,2,1,0:T(8,128)(2,1)S(1)}, bf16[6,1,24,256]{3,2,1,0:T(8,128)(2,1)S(1)}, u32[]{:S(2)}, u32[]{:S(2)}) collective-permute-start(bf16[6,1,24,256]{3,2,1,0:T(8,128)(2,1)S(1)} %get-tuple-element.395), channel_id=1, source_target_pairs={{0,8},{8,16},{16,24},{1,9},{9,17},{17,25},{2,10},{10,18},{18,26},{... | collective-permute-start | bytes 221192 | tf_op jit(solution)/shard_map/ppermute | solution.py:41
  100.5 15.7 %collective-permute-start.4 = (bf16[6,18,1,256]{3,2,1,0:T(2,128)(2,1)S(1)}, bf16[6,18,1,256]{3,2,1,0:T(2,128)(2,1)S(1)}, u32[]{:S(2)}, u32[]{:S(2)}) collective-permute-start(bf16[6,18,1,256]{3,2,1,0:T(2,128)(2,1)S(1)} %get-tuple-element.375), channel_id=1, source_target_pairs={{1,0},{2,1},{3,2},{4,3},{5,4},{6,5},{7,6},{9,8},{10,9},{11,10},{12... | collective-permute-start | bytes 165896 | tf_op jit(solution)/shard_map/ppermute | solution.py:42
  113.1 3.7 %collective-permute-start.3 = (bf16[6,18,1,256]{3,2,1,0:T(2,128)(2,1)S(1)}, bf16[6,18,1,256]{3,2,1,0:T(2,128)(2,1)S(1)}, u32[]{:S(2)}, u32[]{:S(2)}) collective-permute-start(bf16[6,18,1,256]{3,2,1,0:T(2,128)(2,1)S(1)} %get-tuple-element.376), channel_id=1, source_target_pairs={{0,1},{1,2},{2,3},{3,4},{4,5},{5,6},{6,7},{8,9},{9,10},{10,11},{11... | collective-permute-start | bytes 165896 | tf_op jit(solution)/shard_map/ppermute | solution.py:41
  131.1 77.6 %copy-start.3 = (f32[256]{0:T(256)S(1)}, f32[256]{0:T(256)}, u32[]{:S(2)}) copy-start(f32[256]{0:T(256)} %param.16) | copy-start | bytes 3076
  131.1 77.6 %copy-start.1 = (f32[256]{0:T(256)S(1)}, f32[256]{0:T(256)}, u32[]{:S(2)}) copy-start(f32[256]{0:T(256)} %param.17) | copy-start | bytes 3076
  209.2 7.2 %collective-permute-start.5 = (bf16[2,16,24,256]{3,2,1,0:T(8,128)(2,1)S(1)}, bf16[2,16,24,256]{3,2,1,0:T(8,128)(2,1)S(1)}, u32[]{:S(2)}, u32[]{:S(2)}) collective-permute-start(bf16[2,16,24,256]{3,2,1,0:T(8,128)(2,1)S(1)} %slice.427), channel_id=1, source_target_pairs={{0,32},{32,64},{64,96},{96,128},{128,160},{160,192},{192,224},{1,3... | collective-permute-start | bytes 1179656 | tf_op jit(solution)/shard_map/ppermute | solution.py:31
  216.5 5.5 %collective-permute-start.7 = (bf16[6,1,24,256]{3,2,1,0:T(8,128)(2,1)S(1)}, bf16[6,1,24,256]{3,2,1,0:T(8,128)(2,1)S(1)}, u32[]{:S(2)}, u32[]{:S(2)}) collective-permute-start(bf16[6,1,24,256]{3,2,1,0:T(8,128)(2,1)S(1)} %get-tuple-element.392), channel_id=1, source_target_pairs={{8,0},{16,8},{24,16},{9,1},{17,9},{25,17},{10,2},{18,10},{26,18},{... | collective-permute-start | bytes 221192 | tf_op jit(solution)/shard_map/ppermute | solution.py:42
  217.8 5.4 %collective-permute-start.6 = (bf16[6,1,24,256]{3,2,1,0:T(8,128)(2,1)S(1)}, bf16[6,1,24,256]{3,2,1,0:T(8,128)(2,1)S(1)}, u32[]{:S(2)}, u32[]{:S(2)}) collective-permute-start(bf16[6,1,24,256]{3,2,1,0:T(8,128)(2,1)S(1)} %get-tuple-element.391), channel_id=1, source_target_pairs={{0,8},{8,16},{16,24},{1,9},{9,17},{17,25},{2,10},{10,18},{18,26},{... | collective-permute-start | bytes 221192 | tf_op jit(solution)/shard_map/ppermute | solution.py:41
  223.3 11.8 %collective-permute-start.9 = (bf16[6,18,1,256]{3,2,1,0:T(2,128)(2,1)S(1)}, bf16[6,18,1,256]{3,2,1,0:T(2,128)(2,1)S(1)}, u32[]{:S(2)}, u32[]{:S(2)}) collective-permute-start(bf16[6,18,1,256]{3,2,1,0:T(2,128)(2,1)S(1)} %get-tuple-element.371), channel_id=1, source_target_pairs={{1,0},{2,1},{3,2},{4,3},{5,4},{6,5},{7,6},{9,8},{10,9},{11,10},{12... | collective-permute-start | bytes 165896 | tf_op jit(solution)/shard_map/ppermute | solution.py:42
  232.2 3.7 %collective-permute-start.8 = (bf16[6,18,1,256]{3,2,1,0:T(2,128)(2,1)S(1)}, bf16[6,18,1,256]{3,2,1,0:T(2,128)(2,1)S(1)}, u32[]{:S(2)}, u32[]{:S(2)}) collective-permute-start(bf16[6,18,1,256]{3,2,1,0:T(2,128)(2,1)S(1)} %get-tuple-element.372), channel_id=1, source_target_pairs={{0,1},{1,2},{2,3},{3,4},{4,5},{5,6},{6,7},{8,9},{9,10},{10,11},{11... | collective-permute-start | bytes 165896 | tf_op jit(solution)/shard_map/ppermute | solution.py:41
  250.4 1.1 copy-start
  250.4 1.1 copy-start.2
where the time goes:
time: 262 us; the launch traced here: 260 us
  blocking collectives  155 us (59%)
  starting transfers between devices  40.1 us (15%)
  local copies, waits for them, and re-layouts  29.3 us (11%)
  matrix products  14.1 us (5%)
  other arithmetic  11.4 us (4%)
  waiting for transfers between devices  8.38 us (3%)
    psum x2, blocking collectives, span_moments(): tile_sum, tile_square = lax.psum((local_sum, local_square), ('row', 'col'))  127 us
    unnamed x2, blocking collectives  27.7 us
    ppermute x4, starting transfers between devices, extended(): after = lax.ppermute(leading, axis, down)  24.1 us
    dot_general x18, matrix products, conv_block(): jnp.dot(stacked.reshape(-1, 3 * channels), kernel[:, tap_row, tap_col].re...  14.1 us
    slice x7, local copies, waits for them, and re-layouts, conv_block(): window[tap_time:tap_time + span_frames]  12.4 us
    ppermute x4, starting transfers between devices, extended(): before = lax.ppermute(last, axis, up)  12 us
  transfers between devices with their start and end apart: 10, of which 6 were waited for; matrix products, arithmetic and copies ran while one was open for 3% of the time, Pallas kernels for 0%

commit v1 on v0

v1 whole, which is shorter than its diff:
```python
import functools

import jax
import jax.numpy as jnp
from jax import lax
from jax.experimental import pallas as pl
from jax.experimental.pallas import tpu as pltpu
from jax.sharding import PartitionSpec as P

GROUPS = 32
EPSILON = 1e-06
MESH = pl.DeviceIdType.MESH
F32 = jnp.float32
BF16 = jnp.bfloat16


def lane_of(shape):
    return lax.broadcasted_iota(jnp.int32, shape, 1) % 8


def group_total(x):
    lane = lane_of(x.shape)
    lanes = x.shape[1]
    for step in (1, 2, 4):
        above = pltpu.roll(x, lanes - step, 1)
        below = pltpu.roll(x, step, 1)
        x = x + jnp.where((lane // step) % 2 == 0, above, below)
    return x


def pack_moments(total, square):
    rows = jnp.concatenate([total[:, :128], total[:, 128:], square[:, :128], square[:, 128:]], axis=0)
    rows = group_total(rows)
    lane = lane_of((1, 128))
    row = jnp.zeros((1, 128), F32)
    for k in range(4):
        row = jnp.where(lane == k, rows[k : k + 1], row)
    return row


def unpack_moments(row):
    lane = lane_of((1, 128))
    rows = jnp.concatenate([jnp.where(lane == k, row, 0.0) for k in range(4)], axis=0)
    rows = group_total(rows)
    total = jnp.concatenate([rows[0:1], rows[1:2]], axis=1)
    square = jnp.concatenate([rows[2:3], rows[3:4]], axis=1)
    return total, square


def half_terms(row, count, gain, bias):
    total, square = unpack_moments(row)
    mean = total / count
    scale = lax.rsqrt(square / count - mean * mean + EPSILON) * gain
    return 0.5 * scale, 0.5 * (bias - mean * scale)


def silu_of(x, scale, offset):
    u = x * scale + offset
    return u + u * jnp.tanh(u)


def build(x_ref, col_ref, act_ref, edge_ref, terms_ref, first, last, before, marks):
    north, south, west, east = marks
    rows = x_ref.shape[1]
    cols = x_ref.shape[2]
    scale = terms_ref[2 * before : 2 * before + 1, :]
    offset = terms_ref[2 * before + 1 : 2 * before + 2, :]
    at = lax.broadcasted_iota(jnp.int32, (col_ref.shape[2], 1), 0)
    inside = jnp.where(at == 0, north, jnp.where(at == rows - 1, south, 1.0))
    place = lax.broadcasted_iota(jnp.int32, (cols, 1), 0)

    @pl.loop(first, last)
    def _(t):
        for side, mark in ((0, west), (1, east)):
            keep = inside * mark
            edge_ref[side] = silu_of(col_ref[side, t].astype(F32), scale * keep, offset * keep)
        for h in range(rows):
            keep = north if h == 0 else south if h == rows - 1 else None
            s, o = (scale, offset) if keep is None else (scale * keep, offset * keep)
            z = silu_of(x_ref[t, h].astype(F32), s, o)
            act_ref[1, t, h] = z.astype(BF16)
            left = jnp.where(place == 0, edge_ref[0, h : h + 1, :], pltpu.roll(z, 1, 0))
            act_ref[0, t, h] = left.astype(BF16)
            right = jnp.where(place == cols - 1, edge_ref[1, h : h + 1, :], pltpu.roll(z, cols - 1, 0))
            act_ref[2, t, h] = right.astype(BF16)


def conv_frame(act_ref, w_ref, t):
    _, _, rows, cols, channels = act_ref.shape
    rows = rows - 2
    out = jnp.zeros((rows * cols, w_ref.shape[-1]), F32)
    for a in range(3):
        for b in range(3):
            for e in range(3):
                x = act_ref[e, t + a, b : b + rows].reshape(rows * cols, channels)
                out = out + jnp.dot(x, w_ref[(a * 3 + b) * 3 + e], preferred_element_type=F32)
    return out


def sums_of(x):
    parts = x.reshape(-1, 8, x.shape[-1])
    return jnp.sum(parts, axis=0), jnp.sum(parts * parts, axis=0)


def marks_of(n_row, n_col):
    row, col = lax.axis_index("row"), lax.axis_index("col")
    one, zero = jnp.float32(1.0), jnp.float32(0.0)
    return (
        jnp.where(row == 0, zero, one),
        jnp.where(row == n_row - 1, zero, one),
        jnp.where(col == 0, zero, one),
        jnp.where(col == n_col - 1, zero, one),
    )


def first_kernel(
    sizes, count,
    lat_hbm, w1_hbm, w2_hbm, gain1_hbm, bias1_hbm, gain2_hbm, bias2_hbm,
    xl, xh, colh, w2, terms2,
    act, w1, coll, send_l, send_h, edge, pick, affine, terms1,
    sum_send, plane_in, tm_send, tm_in,
    load_sem, send_sem, recv_sem, sum_send_sem, sum_recv_sem,
):
    n_tm, n_row, n_col = sizes
    tm, row, col = lax.axis_index("tm"), lax.axis_index("row"), lax.axis_index("col")
    frames, rows, cols = xl.shape[0] - 2, xl.shape[1] - 2, xl.shape[2]
    plane = n_row * n_col
    mine = row * n_col + col
    marks = marks_of(n_row, n_col)

    loads = [
        pltpu.make_async_copy(lat_hbm, xl.at[2:, 1 : rows + 1], load_sem.at[0]),
        pltpu.make_async_copy(gain1_hbm, affine.at[0], load_sem.at[1]),
        pltpu.make_async_copy(bias1_hbm, affine.at[1], load_sem.at[2]),
        pltpu.make_async_copy(gain2_hbm, affine.at[2], load_sem.at[3]),
        pltpu.make_async_copy(bias2_hbm, affine.at[3], load_sem.at[4]),
        pltpu.make_async_copy(w1_hbm, w1, load_sem.at[5]),
        pltpu.make_async_copy(w2_hbm, w2, load_sem.at[6]),
    ]
    for load in loads:
        load.start()

    def plane_peer(d):
        at = lax.rem(mine + d, plane)
        return (tm, at // n_col, lax.rem(at, n_col))

    def tm_peer(d):
        return (lax.rem(tm + d, n_tm), row, col)

    barrier = pltpu.get_barrier_semaphore()

    @pl.loop(1, plane)
    def _(d):
        pl.semaphore_signal(barrier, inc=1, device_id=plane_peer(d), device_id_type=MESH)

    @pl.loop(1, n_tm)
    def _(d):
        pl.semaphore_signal(barrier, inc=1, device_id=tm_peer(d), device_id_type=MESH)

    pick[...] = jnp.zeros_like(pick)
    north = (tm, lax.rem(row + n_row - 1, n_row), col)
    south = (tm, lax.rem(row + 1, n_row), col)
    west = (tm, row, lax.rem(col + n_col - 1, n_col))
    east = (tm, row, lax.rem(col + 1, n_col))
    later = tm_peer(1)

    def remote(src, dst, which, device):
        copy = pltpu.make_async_remote_copy(
            src_ref=src, dst_ref=dst, send_sem=send_sem.at[which], recv_sem=recv_sem.at[which],
            device_id=device, device_id_type=MESH,
        )
        copy.start()
        return copy

    def send_plane(which, moments):
        sum_send[which] = moments

        @pl.loop(1, plane)
        def _(d):
            pltpu.make_async_remote_copy(
                src_ref=sum_send.at[which], dst_ref=plane_in.at[which, d - 1],
                send_sem=sum_send_sem.at[which], recv_sem=sum_recv_sem.at[which],
                device_id=plane_peer(d), device_id_type=MESH,
            ).start()

    def all_plane(which):
        pltpu.make_async_copy(plane_in.at[which], plane_in.at[which], sum_recv_sem.at[which]).wait()
        return sum_send[which] + jnp.sum(plane_in[which], axis=0)

    def send_tm(which, moments):
        tm_send[which] = moments

        @pl.loop(1, n_tm)
        def _(d):
            pltpu.make_async_remote_copy(
                src_ref=tm_send.at[which], dst_ref=tm_in.at[which, d - 1],
                send_sem=sum_send_sem.at[2 + which], recv_sem=sum_recv_sem.at[2 + which],
                device_id=tm_peer(d), device_id_type=MESH,
            ).start()

    def all_tm(which, terms):
        pltpu.make_async_copy(tm_in.at[which], tm_in.at[which], sum_recv_sem.at[2 + which]).wait()
        prior = jnp.zeros((1, 128), F32)
        for d in range(1, n_tm):
            prior = prior + jnp.where(tm >= d, tm_in[which, d - 1], 0.0)
        upto = prior + tm_send[which]
        done = tm.astype(F32)
        gain, bias = affine[2 * which], affine[2 * which + 1]
        scale, offset = half_terms(upto, (done + 1.0) * count, gain, bias)
        terms[0:1, :] = scale
        terms[1:2, :] = offset
        scale, offset = half_terms(prior, jnp.maximum(done, 1.0) * count, gain, bias)
        keep = jnp.where(tm == 0, jnp.float32(0.0), jnp.float32(1.0))
        terms[2:3, :] = scale * keep
        terms[3:4, :] = offset * keep

    def sums_sent(which):
        pltpu.make_async_copy(plane_in.at[which], plane_in.at[which], sum_send_sem.at[which]).wait()
        pltpu.make_async_copy(tm_in.at[which], tm_in.at[which], sum_send_sem.at[2 + which]).wait()

    def columns(x, out):
        for side, lo, at in ((0, cols - 8, 7), (1, 0, 0)):
            @pl.loop(2, frames + 2)
            def _(t):
                for h in range(rows + 2):
                    tile = x[t, h, lo : lo + 8, :].astype(F32)
                    pick[h : h + 1, :] = tile[at : at + 1, :]
                out[side, t - 2] = pick[...].astype(BF16)

    def halo_rows(x, base, lo, hi):
        return [
            remote(x.at[lo:hi, 1], x.at[lo:hi, rows + 1], base, north),
            remote(x.at[lo:hi, rows], x.at[lo:hi, 0], base + 1, south),
        ]

    def halo_columns(out, cells, base):
        return [
            remote(out.at[0], cells.at[0, 2:], base, east),
            remote(out.at[1], cells.at[1, 2:], base + 1, west),
        ]

    def onward_rows(x, base):
        return [
            remote(x.at[frames : frames + 2, 0], x.at[0:2, 0], base, later),
            remote(x.at[frames : frames + 2, rows + 1], x.at[0:2, rows + 1], base + 1, later),
        ]

    def onward_columns(cells, base):
        return [
            remote(cells.at[0, frames : frames + 2], cells.at[0, 0:2], base, later),
            remote(cells.at[1, frames : frames + 2], cells.at[1, 0:2], base + 1, later),
        ]

    def onward_frames(x, which):
        return [remote(x.at[frames : frames + 2, 1 : rows + 1], x.at[0:2, 1 : rows + 1], which, later)]

    loads[0].wait()

    def add_frame(t, so_far):
        s, q = sums_of(xl[t, 1 : rows + 1].reshape(rows * cols, -1).astype(F32))
        return so_far[0] + s, so_far[1] + q

    none = jnp.zeros((8, xl.shape[-1]), F32)
    s, q = lax.fori_loop(2, frames + 2, add_frame, (none, none))
    moments = pack_moments(jnp.sum(s, axis=0, keepdims=True), jnp.sum(q, axis=0, keepdims=True))
    pl.semaphore_wait(barrier, plane - 1 + n_tm - 1)

    send_plane(0, moments)
    by_row = halo_rows(xl, 0, 2, frames + 2)
    onward = onward_frames(xl, 2)
    for copy in by_row:
        copy.wait_recv()
    columns(xl, send_l)
    by_col = halo_columns(send_l, coll, 3)
    onward += onward_rows(xl, 5)
    moments = all_plane(0)
    send_tm(0, moments)
    for copy in by_col:
        copy.wait_recv()
    onward += onward_columns(coll, 7)
    for load in loads[1:5]:
        load.wait()
    all_tm(0, terms1)

    build(xl, coll, act, edge, terms1, 2, frames + 2, 0, marks)
    loads[5].wait()

    def hidden_frame(t, so_far):
        h = conv_frame(act, w1, t).astype(BF16)
        xh[t + 2, 1 : rows + 1] = h.reshape(rows, cols, -1)
        s, q = sums_of(h.astype(F32))
        return so_far[0] + s, so_far[1] + q

    sums = lax.fori_loop(frames - 2, frames, hidden_frame, (none, none))
    onward2 = onward_frames(xh, 9)
    by_row2 = halo_rows(xh, 10, frames, frames + 2)
    for copy in onward:
        copy.wait_recv()
    build(xl, coll, act, edge, terms1, 0, 2, 1, marks)
    s, q = lax.fori_loop(0, frames - 2, hidden_frame, sums)
    moments = pack_moments(jnp.sum(s, axis=0, keepdims=True), jnp.sum(q, axis=0, keepdims=True))
    send_plane(1, moments)
    by_row2 += halo_rows(xh, 12, 2, frames)
    for copy in by_row2:
        copy.wait_recv()
    columns(xh, send_h)
    by_col2 = halo_columns(send_h, colh, 14)
    onward2 += onward_rows(xh, 16)
    moments = all_plane(1)
    send_tm(1, moments)
    for copy in by_col2:
        copy.wait_recv()
    onward2 += onward_columns(colh, 18)
    all_tm(1, terms2)
    loads[6].wait()
    for copy in onward2:
        copy.wait_recv()
    for copy in by_row + by_col + onward + by_row2 + by_col2 + onward2:
        copy.wait_send()
    sums_sent(0)
    sums_sent(1)


N_COPIES = 20


def second_kernel(
    sizes, xl, xh, colh, w2, terms2, bias_ref, out_hbm, act, edge, wide, stage, out_sem
):
    n_tm, n_row, n_col = sizes
    marks = marks_of(n_row, n_col)
    frames, rows, cols = xl.shape[0] - 2, xl.shape[1] - 2, xl.shape[2]
    build(xh, colh, act, edge, terms2, 2, frames + 2, 0, marks)
    build(xh, colh, act, edge, terms2, 0, 2, 1, marks)

    def stores(t):
        return [
            pltpu.make_async_copy(stage.at[t], out_hbm.at[t, :, k], out_sem.at[t, k]) for k in range(2)
        ]

    for t in range(frames):
        y = conv_frame(act, w2, t) + bias_ref[...]
        y = y + xl[t + 2, 1 : rows + 1].reshape(rows * cols, -1).astype(F32)
        for half in range(2):
            part = y[:, 128 * half : 128 * half + 128]
            wide[t % 2, half, pl.ds(0, rows * cols, stride=2), :] = part
            wide[t % 2, half, pl.ds(1, rows * cols, stride=2), :] = part
        for half in range(2):
            stage[t, :, :, 128 * half : 128 * half + 128] = (
                wide[t % 2, half].astype(BF16).reshape(rows, 2 * cols, 128)
            )
        for copy in stores(t):
            copy.start()
    for t in range(frames):
        for copy in stores(t):
            copy.wait()


def on_device(sizes, latent, gain_first, bias_first, kernel_first, gain_second, bias_second, kernel_second, conv_bias):
    n_tm, n_row, n_col = sizes
    frames, rows, cols, channels = latent.shape
    plane = n_row * n_col
    per_span = float(frames * rows * n_row * cols * n_col * (channels // GROUPS))
    tile = (frames + 2, rows + 2, cols, channels)
    tall = -(-(rows + 2) // 8) * 8
    cells = (2, frames + 2, tall, channels)
    send = (2, frames, tall, channels)
    taps = (27, channels, channels)
    anywhere = pl.BlockSpec(memory_space=pl.ANY)
    inside = pl.BlockSpec(memory_space=pltpu.VMEM)
    kept = [
        pltpu.VMEM(tile, BF16),
        pltpu.VMEM(tile, BF16),
        pltpu.VMEM(cells, BF16),
        pltpu.VMEM(taps, BF16),
        pltpu.VMEM((8, channels), F32),
    ]
    held = pl.pallas_call(
        functools.partial(first_kernel, sizes, per_span),
        out_shape=kept,
        in_specs=[anywhere] * 7,
        out_specs=[inside] * 5,
        scratch_shapes=[
            pltpu.VMEM((3, *tile), BF16),
            pltpu.VMEM(taps, BF16),
            pltpu.VMEM(cells, BF16),
            pltpu.VMEM(send, BF16),
            pltpu.VMEM(send, BF16),
            pltpu.VMEM((2, tall, channels), F32),
            pltpu.VMEM((tall, channels), F32),
            pltpu.VMEM((4, 1, channels), F32),
            pltpu.VMEM((8, channels), F32),
            pltpu.VMEM((2, 1, 128), F32),
            pltpu.VMEM((2, plane - 1, 1, 128), F32),
            pltpu.VMEM((2, 1, 128), F32),
            pltpu.VMEM((2, n_tm - 1, 1, 128), F32),
            pltpu.SemaphoreType.DMA((7,)),
            pltpu.SemaphoreType.DMA((N_COPIES,)),
            pltpu.SemaphoreType.DMA((N_COPIES,)),
            pltpu.SemaphoreType.DMA((4,)),
            pltpu.SemaphoreType.DMA((4,)),
        ],
        compiler_params=pltpu.CompilerParams(
            collective_id=0, has_side_effects=True, vmem_limit_bytes=24 * 2**20
        ),
        name="first_conv",
    )(
        latent,
        kernel_first.reshape(taps),
        kernel_second.reshape(taps),
        gain_first.reshape(1, channels),
        bias_first.reshape(1, channels),
        gain_second.reshape(1, channels),
        bias_second.reshape(1, channels),
    )
    out = pl.pallas_call(
        functools.partial(second_kernel, sizes),
        out_shape=jax.ShapeDtypeStruct((frames, rows, 2, 2 * cols, channels), BF16),
        in_specs=[inside] * 6,
        out_specs=anywhere,
        scratch_shapes=[
            pltpu.VMEM((3, *tile), BF16),
            pltpu.VMEM((2, tall, channels), F32),
            pltpu.VMEM((2, 2, 2 * rows * cols, 128), F32),
            pltpu.VMEM((frames, rows, 2 * cols, channels), BF16),
            pltpu.SemaphoreType.DMA((frames, 2)),
        ],
        compiler_params=pltpu.CompilerParams(vmem_limit_bytes=24 * 2**20),
        name="second_conv",
    )(*held, conv_bias.reshape(1, channels))
    return out.reshape(frames, 2 * rows, 2 * cols, channels)


def solution(mesh):
    sizes = (mesh.shape["tm"], mesh.shape["row"], mesh.shape["col"])
    return jax.shard_map(
        functools.partial(on_device, sizes),
        mesh=mesh,
        in_specs=(P("tm", "row", "col", None), P(), P(), P(), P(), P(), P(), P()),
        out_specs=P("tm", "row", "col", None),
        check_vma=False,
    )
```

time: 262 us -> 59.4 us (0.23)
  blocking collectives: 155 us -> 0 us
  Pallas kernels: 0 us -> 51.3 us
  starting transfers between devices: 40.1 us -> 0 us
  local copies, waits for them, and re-layouts: 29.3 us -> 7.85 us
  matrix products: 14.1 us -> 0 us
  other arithmetic: 11.4 us -> 0 us
  waiting for transfers between devices: 8.38 us -> 0 us
    psum x2 -> x0, blocking collectives: 127 us -> none  [span_moments(): tile_sum, tile_square = lax.psum((local_sum, local_square), ('row', 'col'))]
    pallas_call x0 -> x2, Pallas kernels: none -> 51.3 us  [the longest x1 42.9 us: on_device(): pl.pallas_call(functools.partial(first_kernel, sizes, per_span), out_shap...]
    ppermute x10 -> x0, starting transfers between devices: 40.1 us -> none  [the longest x4 24.1 us: extended(): after = lax.ppermute(leading, axis, down)]
    unnamed x2 -> x0, blocking collectives: 27.7 us -> none
    slice x11 -> x0, local copies, waits for them, and re-layouts: 17.1 us -> none  [the longest x7 12.4 us: conv_block(): window[tap_time:tap_time + span_frames]]
    dot_general x18 -> x0, matrix products: 14.1 us -> none  [conv_block(): jnp.dot(stacked.reshape(-1, 3 * channels), kernel[:, tap_row, tap_col].re...]
    ppermute x10 -> x0, waiting for transfers between devices: 8.38 us -> none  [the longest x2 4.7 us: from_behind(): return lax.ppermute(block, axis, route)]
    concatenate x24 -> x0, other arithmetic: 6.25 us -> none  [the longest x6 3.22 us: extended(): x = jnp.concatenate([before, x, after], axis=dim)]
  transfers between devices with their start and end apart: 10 -> 0, of which waited for: 6 -> 0; matrix products, arithmetic and copies ran while one was open for 3% -> 0% of each run, Pallas kernels for 0% -> 0%
where the time goes in v1:
time: 59.4 us; the launch traced here: 59.2 us
  Pallas kernels  51.3 us (86%)
  local copies, waits for them, and re-layouts  7.85 us (13%)
    pallas_call x1, Pallas kernels, on_device(): pl.pallas_call(functools.partial(first_kernel, sizes, per_span), out_shap...  42.9 us
    pallas_call x1, Pallas kernels, on_device(): pl.pallas_call(functools.partial(second_kernel, sizes), out_shape=jax.Sha...  8.39 us
    unnamed x16, local copies, waits for them, and re-layouts  7.85 us

profile of v1, /device:TPU:1, one launch (start us, length us, event | category | flops | bytes accessed | tf_op | source)
XLA Modules:
  0.0 59.2 jit_solution(4185503853917897747)
XLA Ops:
  0.0 0.0 copy-start
  0.0 2.0 %copy-done = bf16[3,3,3,256,256]{4,3,2,1,0:T(8,128)(2,1)S(1)} copy-done((bf16[3,3,3,256,256]{4,3,2,1,0:T(8,128)(2,1)S(1)}, bf16[3,3,3,256,256]{4,3,2,1,0:T(8,128)(2,1)}, u32[]{:S(2)}) %copy-start) | copy-done | bytes 3538968
  2.0 0.0 copy-start.1
  2.0 2.0 %copy-done.1 = bf16[3,3,3,256,256]{4,3,2,1,0:T(8,128)(2,1)S(1)} copy-done((bf16[3,3,3,256,256]{4,3,2,1,0:T(8,128)(2,1)S(1)}, bf16[3,3,3,256,256]{4,3,2,1,0:T(8,128)(2,1)}, u32[]{:S(2)}) %copy-start.1) | copy-done | bytes 3538968
  4.0 0.0 copy-start.2
  4.0 1.1 %copy-done.2 = bf16[4,16,24,256]{3,2,1,0:T(8,128)(2,1)S(1)} copy-done((bf16[4,16,24,256]{3,2,1,0:T(8,128)(2,1)S(1)}, bf16[4,16,24,256]{3,2,1,0:T(8,128)(2,1)}, u32[]{:S(2)}) %copy-start.2) | copy-done | bytes 786456
  5.1 0.0 copy-start.3
  5.1 0.7 %copy-done.3 = f32[256]{0:T(256)S(1)} copy-done((f32[256]{0:T(256)S(1)}, f32[256]{0:T(256)}, u32[]{:S(2)}) %copy-start.3) | copy-done | bytes 1048
  5.8 0.0 copy-start.4
  5.8 0.7 %copy-done.4 = f32[256]{0:T(256)S(1)} copy-done((f32[256]{0:T(256)S(1)}, f32[256]{0:T(256)}, u32[]{:S(2)}) %copy-start.4) | copy-done | bytes 1048
  6.5 0.0 copy-start.5
  6.5 0.7 %copy-done.5 = f32[256]{0:T(256)S(1)} copy-done((f32[256]{0:T(256)S(1)}, f32[256]{0:T(256)}, u32[]{:S(2)}) %copy-start.5) | copy-done | bytes 1048
  7.2 0.0 copy-start.6
  7.2 0.7 %copy-done.6 = f32[256]{0:T(256)S(1)} copy-done((f32[256]{0:T(256)S(1)}, f32[256]{0:T(256)}, u32[]{:S(2)}) %copy-start.6) | copy-done | bytes 1048
  7.9 0.0 copy-start.7
  7.9 42.9 %first_conv.1 = (bf16[6,18,24,256]{3,2,1,0:T(8,128)(2,1)S(1)}, bf16[6,18,24,256]{3,2,1,0:T(8,128)(2,1)S(1)}, bf16[2,6,24,256]{3,2,1,0:T(8,128)(2,1)S(1)}, bf16[27,256,256]{2,1,0:T(8,128)(2,1)S(1)}, f32[8,256]{1,0:T(8,128)S(1)}) custom-call(bf16[4,16,24,256]{3,2,1,0:T(8,128)(2,1)S(1)} %copy-done.2, bf16[27,256,256]{2,1,0:T(8,128)(2,1)S(1)} %bitcast.8, ...), custom_call_target="tpu_custom_call" | custom-call | tf_op jit(solution)/shard_map/first_conv/pallas_call | solution.py:378
  50.8 0.0 copy-done.7
  50.8 8.4 %second_conv.1 = bf16[4,16,2,48,256]{4,3,2,1,0:T(8,128)(2,1)} custom-call(bf16[6,18,24,256]{3,2,1,0:T(8,128)(2,1)S(1)} %get-tuple-element.10.xl, bf16[6,18,24,256]{3,2,1,0:T(8,128)(2,1)S(1)} %get-tuple-element.11.xh, bf16[2,6,24,256]{3,2,1,0:T(8,128)(2,1)S(1)} %get-tuple-element.12.colh, bf16[27,256,256]{2,1,0:T(8,128)(2,1)S(1)} %get-tuple-element.13.w2, ...), custom_call_target="tpu_custom_call" | custom-call | tf_op jit(solution)/shard_map/second_conv/pallas_call | solution.py:416
Async XLA Ops:
  0.0 2.0 %copy-start = (bf16[3,3,3,256,256]{4,3,2,1,0:T(8,128)(2,1)S(1)}, bf16[3,3,3,256,256]{4,3,2,1,0:T(8,128)(2,1)}, u32[]{:S(2)}) copy-start(bf16[3,3,3,256,256]{4,3,2,1,0:T(8,128)(2,1)} %param.11) | copy-start | bytes 10616836
  2.0 2.0 %copy-start.1 = (bf16[3,3,3,256,256]{4,3,2,1,0:T(8,128)(2,1)S(1)}, bf16[3,3,3,256,256]{4,3,2,1,0:T(8,128)(2,1)}, u32[]{:S(2)}) copy-start(bf16[3,3,3,256,256]{4,3,2,1,0:T(8,128)(2,1)} %param.14) | copy-start | bytes 10616836
  4.0 1.1 %copy-start.2 = (bf16[4,16,24,256]{3,2,1,0:T(8,128)(2,1)S(1)}, bf16[4,16,24,256]{3,2,1,0:T(8,128)(2,1)}, u32[]{:S(2)}) copy-start(bf16[4,16,24,256]{3,2,1,0:T(8,128)(2,1)} %lat_hbm.1) | copy-start | bytes 2359300
  5.1 0.7 %copy-start.3 = (f32[256]{0:T(256)S(1)}, f32[256]{0:T(256)}, u32[]{:S(2)}) copy-start(f32[256]{0:T(256)} %param.9) | copy-start | bytes 3076
  5.8 0.7 %copy-start.4 = (f32[256]{0:T(256)S(1)}, f32[256]{0:T(256)}, u32[]{:S(2)}) copy-start(f32[256]{0:T(256)} %param.10) | copy-start | bytes 3076
  6.5 0.7 %copy-start.5 = (f32[256]{0:T(256)S(1)}, f32[256]{0:T(256)}, u32[]{:S(2)}) copy-start(f32[256]{0:T(256)} %param.12) | copy-start | bytes 3076
  7.2 0.7 %copy-start.6 = (f32[256]{0:T(256)S(1)}, f32[256]{0:T(256)}, u32[]{:S(2)}) copy-start(f32[256]{0:T(256)} %param.13) | copy-start | bytes 3076
  7.9 42.9 %copy-start.7 = (f32[256]{0:T(256)S(1)}, f32[256]{0:T(256)}, u32[]{:S(2)}) copy-start(f32[256]{0:T(256)} %param.15) | copy-start | bytes 3076

commit v2 on v1

--- a/solution.py
+++ b/solution.py
@@ -366,7 +366,7 @@
     cells = (2, frames + 2, tall, channels)
     send = (2, frames, tall, channels)
     taps = (27, channels, channels)
-    anywhere = pl.BlockSpec(memory_space=pl.ANY)
+    anywhere = pl.BlockSpec(memory_space=pltpu.HBM)
     inside = pl.BlockSpec(memory_space=pltpu.VMEM)
     kept = [
         pltpu.VMEM(tile, BF16),
@@ -405,13 +405,18 @@
         ),
         name="first_conv",
     )(
-        latent,
-        kernel_first.reshape(taps),
-        kernel_second.reshape(taps),
-        gain_first.reshape(1, channels),
-        bias_first.reshape(1, channels),
-        gain_second.reshape(1, channels),
-        bias_second.reshape(1, channels),
+        *(
+            pltpu.with_memory_space_constraint(x, pltpu.HBM)
+            for x in (
+                latent,
+                kernel_first.reshape(taps),
+                kernel_second.reshape(taps),
+                gain_first.reshape(1, channels),
+                bias_first.reshape(1, channels),
+                gain_second.reshape(1, channels),
+                bias_second.reshape(1, channels),
+            )
+        )
     )
     out = pl.pallas_call(
         functools.partial(second_kernel, sizes),

time: 59.4 us -> 50.5 us (0.85)
  local copies, waits for them, and re-layouts: 7.85 us -> 0.01 us
  Pallas kernels: 51.3 us -> 50.4 us
    unnamed x16 -> x2, local copies, waits for them, and re-layouts: 7.85 us -> 0.01 us
    pallas_call x1, Pallas kernels: 42.9 us -> 42.1 us  [on_device(): pl.pallas_call(functools.partial(first_kernel, sizes, per_span), out_shap...]
where the time goes in v2:
time: 50.5 us
  Pallas kernels  50.4 us (100%)
    pallas_call x1, Pallas kernels, on_device(): pl.pallas_call(functools.partial(first_kernel, sizes, per_span), out_shap...  42.1 us
    pallas_call x1, Pallas kernels, on_device(): pl.pallas_call(functools.partial(second_kernel, sizes), out_shape=jax.Sha...  8.39 us

profile of v2, /device:TPU:1, one launch (start us, length us, event | category | flops | bytes accessed | tf_op | source)
XLA Modules:
  0.0 50.5 jit_solution(903915815920996551)
XLA Ops:
  0.0 0.0 copy-start
  0.0 42.1 %first_conv.1 = (bf16[6,18,24,256]{3,2,1,0:T(8,128)(2,1)S(1)}, bf16[6,18,24,256]{3,2,1,0:T(8,128)(2,1)S(1)}, bf16[2,6,24,256]{3,2,1,0:T(8,128)(2,1)S(1)}, bf16[27,256,256]{2,1,0:T(8,128)(2,1)S(1)}, f32[8,256]{1,0:T(8,128)S(1)}) custom-call(bf16[4,16,24,256]{3,2,1,0:T(8,128)(2,1)} %lat_hbm.1, bf16[27,256,256]{2,1,0:T(8,128)(2,1)} %bitcast.9, ...), custom_call_target="tpu_custom_call" | custom-call | tf_op jit(solution)/shard_map/first_conv/pallas_call | solution.py:378
  42.1 0.0 copy-done
  42.1 8.4 %second_conv.1 = bf16[4,16,2,48,256]{4,3,2,1,0:T(8,128)(2,1)} custom-call(bf16[6,18,24,256]{3,2,1,0:T(8,128)(2,1)S(1)} %get-tuple-element.10.xl, bf16[6,18,24,256]{3,2,1,0:T(8,128)(2,1)S(1)} %get-tuple-element.11.xh, bf16[2,6,24,256]{3,2,1,0:T(8,128)(2,1)S(1)} %get-tuple-element.12.colh, bf16[27,256,256]{2,1,0:T(8,128)(2,1)S(1)} %get-tuple-element.13.w2, ...), custom_call_target="tpu_custom_call" | custom-call | tf_op jit(solution)/shard_map/second_conv/pallas_call | solution.py:421
Async XLA Ops:
  0.0 42.1 %copy-start = (f32[256]{0:T(256)S(1)}, f32[256]{0:T(256)}, u32[]{:S(2)}) copy-start(f32[256]{0:T(256)} %param.15) | copy-start | bytes 3076

commit v3 on v2

--- a/solution.py
+++ b/solution.py
@@ -137,7 +137,7 @@
         pltpu.make_async_copy(w1_hbm, w1, load_sem.at[5]),
         pltpu.make_async_copy(w2_hbm, w2, load_sem.at[6]),
     ]
-    for load in loads:
+    for load in loads[:5]:
         load.start()
 
     def plane_peer(d):
@@ -183,9 +183,19 @@
                 device_id=plane_peer(d), device_id_type=MESH,
             ).start()
 
-    def all_plane(which):
+    def all_plane(which, terms):
         pltpu.make_async_copy(plane_in.at[which], plane_in.at[which], sum_recv_sem.at[which]).wait()
-        return sum_send[which] + jnp.sum(plane_in[which], axis=0)
+        both = sum_send[which] + jnp.sum(plane_in[which], axis=0)
+        done = tm.astype(F32)
+        gain, bias = affine[2 * which], affine[2 * which + 1]
+        scale, offset = half_terms(both, (done + 1.0) * count, gain, bias)
+        terms[0:1, :] = scale
+        terms[1:2, :] = offset
+        prior = pltpu.roll(both, 124, 1)
+        scale, offset = half_terms(prior, jnp.maximum(done, 1.0) * count, gain, bias)
+        keep = jnp.where(tm == 0, jnp.float32(0.0), jnp.float32(1.0))
+        terms[2:3, :] = scale * keep
+        terms[3:4, :] = offset * keep
 
     def send_tm(which, moments):
         tm_send[which] = moments
@@ -198,21 +208,12 @@
                 device_id=tm_peer(d), device_id_type=MESH,
             ).start()
 
-    def all_tm(which, terms):
+    def all_tm(which):
         pltpu.make_async_copy(tm_in.at[which], tm_in.at[which], sum_recv_sem.at[2 + which]).wait()
         prior = jnp.zeros((1, 128), F32)
         for d in range(1, n_tm):
             prior = prior + jnp.where(tm >= d, tm_in[which, d - 1], 0.0)
-        upto = prior + tm_send[which]
-        done = tm.astype(F32)
-        gain, bias = affine[2 * which], affine[2 * which + 1]
-        scale, offset = half_terms(upto, (done + 1.0) * count, gain, bias)
-        terms[0:1, :] = scale
-        terms[1:2, :] = offset
-        scale, offset = half_terms(prior, jnp.maximum(done, 1.0) * count, gain, bias)
-        keep = jnp.where(tm == 0, jnp.float32(0.0), jnp.float32(1.0))
-        terms[2:3, :] = scale * keep
-        terms[3:4, :] = offset * keep
+        return prior + tm_send[which] + pltpu.roll(prior, 4, 1)
 
     def sums_sent(which):
         pltpu.make_async_copy(plane_in.at[which], plane_in.at[which], sum_send_sem.at[which]).wait()
@@ -251,10 +252,12 @@
             remote(cells.at[1, frames : frames + 2], cells.at[1, 0:2], base + 1, later),
         ]
 
-    def onward_frames(x, which):
-        return [remote(x.at[frames : frames + 2, 1 : rows + 1], x.at[0:2, 1 : rows + 1], which, later)]
+    def onward_frames(x, which, lo, hi):
+        return [remote(x.at[frames + lo : frames + hi, 1 : rows + 1], x.at[lo:hi, 1 : rows + 1], which, later)]
 
     loads[0].wait()
+    for load in loads[5:]:
+        load.start()
 
     def add_frame(t, so_far):
         s, q = sums_of(xl[t, 1 : rows + 1].reshape(rows * cols, -1).astype(F32))
@@ -265,22 +268,21 @@
     moments = pack_moments(jnp.sum(s, axis=0, keepdims=True), jnp.sum(q, axis=0, keepdims=True))
     pl.semaphore_wait(barrier, plane - 1 + n_tm - 1)
 
-    send_plane(0, moments)
+    send_tm(0, moments)
     by_row = halo_rows(xl, 0, 2, frames + 2)
-    onward = onward_frames(xl, 2)
+    onward = onward_frames(xl, 2, 0, 2)
     for copy in by_row:
         copy.wait_recv()
     columns(xl, send_l)
     by_col = halo_columns(send_l, coll, 3)
     onward += onward_rows(xl, 5)
-    moments = all_plane(0)
-    send_tm(0, moments)
+    send_plane(0, all_tm(0))
     for copy in by_col:
         copy.wait_recv()
     onward += onward_columns(coll, 7)
     for load in loads[1:5]:
         load.wait()
-    all_tm(0, terms1)
+    all_plane(0, terms1)
 
     build(xl, coll, act, edge, terms1, 2, frames + 2, 0, marks)
     loads[5].wait()
@@ -291,27 +293,28 @@
         s, q = sums_of(h.astype(F32))
         return so_far[0] + s, so_far[1] + q
 
-    sums = lax.fori_loop(frames - 2, frames, hidden_frame, (none, none))
-    onward2 = onward_frames(xh, 9)
+    sums = hidden_frame(frames - 2, (none, none))
+    onward2 = onward_frames(xh, 9, 0, 1)
+    sums = hidden_frame(frames - 1, sums)
     by_row2 = halo_rows(xh, 10, frames, frames + 2)
     for copy in onward:
         copy.wait_recv()
     build(xl, coll, act, edge, terms1, 0, 2, 1, marks)
     s, q = lax.fori_loop(0, frames - 2, hidden_frame, sums)
     moments = pack_moments(jnp.sum(s, axis=0, keepdims=True), jnp.sum(q, axis=0, keepdims=True))
-    send_plane(1, moments)
+    send_tm(1, moments)
+    onward2 += onward_frames(xh, 20, 1, 2)
     by_row2 += halo_rows(xh, 12, 2, frames)
     for copy in by_row2:
         copy.wait_recv()
     columns(xh, send_h)
     by_col2 = halo_columns(send_h, colh, 14)
     onward2 += onward_rows(xh, 16)
-    moments = all_plane(1)
-    send_tm(1, moments)
+    send_plane(1, all_tm(1))
     for copy in by_col2:
         copy.wait_recv()
     onward2 += onward_columns(colh, 18)
-    all_tm(1, terms2)
+    all_plane(1, terms2)
     loads[6].wait()
     for copy in onward2:
         copy.wait_recv()
@@ -321,7 +324,7 @@
     sums_sent(1)
 
 
-N_COPIES = 20
+N_COPIES = 21
 
 
 def second_kernel(

time: 50.5 us -> 49.1 us (0.972)
  Pallas kernels: 50.4 us -> 49 us
    pallas_call x1, Pallas kernels: 42.1 us -> 40.6 us  [on_device(): pl.pallas_call(functools.partial(first_kernel, sizes, per_span), out_shap...]
where the time goes in v3:
time: 49.1 us; the launch traced here: 49 us
  Pallas kernels  49 us (100%)
    pallas_call x1, Pallas kernels, on_device(): pl.pallas_call(functools.partial(first_kernel, sizes, per_span), out_shap...  40.6 us
    pallas_call x1, Pallas kernels, on_device(): pl.pallas_call(functools.partial(second_kernel, sizes), out_shape=jax.Sha...  8.39 us

profile of v3, /device:TPU:1, one launch (start us, length us, event | category | flops | bytes accessed | tf_op | source)
XLA Modules:
  0.0 49.0 jit_solution(9666048587374863058)
XLA Ops:
  0.0 0.0 copy-start
  0.0 40.6 %first_conv.1 = (bf16[6,18,24,256]{3,2,1,0:T(8,128)(2,1)S(1)}, bf16[6,18,24,256]{3,2,1,0:T(8,128)(2,1)S(1)}, bf16[2,6,24,256]{3,2,1,0:T(8,128)(2,1)S(1)}, bf16[27,256,256]{2,1,0:T(8,128)(2,1)S(1)}, f32[8,256]{1,0:T(8,128)S(1)}) custom-call(bf16[4,16,24,256]{3,2,1,0:T(8,128)(2,1)} %lat_hbm.1, bf16[27,256,256]{2,1,0:T(8,128)(2,1)} %bitcast.9, ...), custom_call_target="tpu_custom_call" | custom-call | tf_op jit(solution)/shard_map/first_conv/pallas_call | solution.py:381
  40.6 0.0 copy-done
  40.6 8.4 %second_conv.1 = bf16[4,16,2,48,256]{4,3,2,1,0:T(8,128)(2,1)} custom-call(bf16[6,18,24,256]{3,2,1,0:T(8,128)(2,1)S(1)} %get-tuple-element.10.xl, bf16[6,18,24,256]{3,2,1,0:T(8,128)(2,1)S(1)} %get-tuple-element.11.xh, bf16[2,6,24,256]{3,2,1,0:T(8,128)(2,1)S(1)} %get-tuple-element.12.colh, bf16[27,256,256]{2,1,0:T(8,128)(2,1)S(1)} %get-tuple-element.13.w2, ...), custom_call_target="tpu_custom_call" | custom-call | tf_op jit(solution)/shard_map/second_conv/pallas_call | solution.py:424
Async XLA Ops:
  0.0 40.6 %copy-start = (f32[256]{0:T(256)S(1)}, f32[256]{0:T(256)}, u32[]{:S(2)}) copy-start(f32[256]{0:T(256)} %param.15) | copy-start | bytes 3076

commit v4 on v3

--- a/solution.py
+++ b/solution.py
@@ -118,14 +118,12 @@
     lat_hbm, w1_hbm, w2_hbm, gain1_hbm, bias1_hbm, gain2_hbm, bias2_hbm,
     xl, xh, colh, w2, terms2,
     act, w1, coll, send_l, send_h, edge, pick, affine, terms1,
-    sum_send, plane_in, tm_send, tm_in,
+    tm_send, tm_in, col_send, col_in, row_send, row_in,
     load_sem, send_sem, recv_sem, sum_send_sem, sum_recv_sem,
 ):
     n_tm, n_row, n_col = sizes
     tm, row, col = lax.axis_index("tm"), lax.axis_index("row"), lax.axis_index("col")
     frames, rows, cols = xl.shape[0] - 2, xl.shape[1] - 2, xl.shape[2]
-    plane = n_row * n_col
-    mine = row * n_col + col
     marks = marks_of(n_row, n_col)
 
     loads = [
@@ -140,22 +138,26 @@
     for load in loads[:5]:
         load.start()
 
-    def plane_peer(d):
-        at = lax.rem(mine + d, plane)
-        return (tm, at // n_col, lax.rem(at, n_col))
-
     def tm_peer(d):
         return (lax.rem(tm + d, n_tm), row, col)
 
+    def col_peer(d):
+        return (tm, row, lax.rem(col + d, n_col))
+
+    def row_peer(d):
+        return (tm, lax.rem(row + d, n_row), col)
+
+    TM, COL, ROW = 0, 1, 2
+    exchanges = (
+        (n_tm, tm_peer, tm_send, tm_in),
+        (n_col, col_peer, col_send, col_in),
+        (n_row, row_peer, row_send, row_in),
+    )
+
     barrier = pltpu.get_barrier_semaphore()
-
-    @pl.loop(1, plane)
-    def _(d):
-        pl.semaphore_signal(barrier, inc=1, device_id=plane_peer(d), device_id_type=MESH)
-
-    @pl.loop(1, n_tm)
-    def _(d):
-        pl.semaphore_signal(barrier, inc=1, device_id=tm_peer(d), device_id_type=MESH)
+    for n, peer, _, _ in exchanges:
+        for d in range(1, n):
+            pl.semaphore_signal(barrier, inc=1, device_id=peer(d), device_id_type=MESH)
 
     pick[...] = jnp.zeros_like(pick)
     north = (tm, lax.rem(row + n_row - 1, n_row), col)
@@ -172,20 +174,27 @@
         copy.start()
         return copy
 
-    def send_plane(which, moments):
-        sum_send[which] = moments
-
-        @pl.loop(1, plane)
-        def _(d):
+    def send_sums(stage, which, sums):
+        n, peer, held, arrived = exchanges[stage]
+        held[which] = sums
+        for d in sorted(range(1, n), key=lambda d: -min(d, n - d)):
             pltpu.make_async_remote_copy(
-                src_ref=sum_send.at[which], dst_ref=plane_in.at[which, d - 1],
-                send_sem=sum_send_sem.at[which], recv_sem=sum_recv_sem.at[which],
-                device_id=plane_peer(d), device_id_type=MESH,
+                src_ref=held.at[which], dst_ref=arrived.at[which, d - 1],
+                send_sem=sum_send_sem.at[2 * stage + which], recv_sem=sum_recv_sem.at[2 * stage + which],
+                device_id=peer(d), device_id_type=MESH,
             ).start()
 
-    def all_plane(which, terms):
-        pltpu.make_async_copy(plane_in.at[which], plane_in.at[which], sum_recv_sem.at[which]).wait()
-        both = sum_send[which] + jnp.sum(plane_in[which], axis=0)
+    def wait_sums(stage, which):
+        arrived = exchanges[stage][3].at[which]
+        pltpu.make_async_copy(arrived, arrived, sum_recv_sem.at[2 * stage + which]).wait()
+
+    def all_along(stage, which):
+        wait_sums(stage, which)
+        held, arrived = exchanges[stage][2:]
+        return held[which] + jnp.sum(arrived[which], axis=0)
+
+    def all_terms(which, terms):
+        both = all_along(ROW, which)
         done = tm.astype(F32)
         gain, bias = affine[2 * which], affine[2 * which + 1]
         scale, offset = half_terms(both, (done + 1.0) * count, gain, bias)
@@ -197,27 +206,17 @@
         terms[2:3, :] = scale * keep
         terms[3:4, :] = offset * keep
 
-    def send_tm(which, moments):
-        tm_send[which] = moments
-
-        @pl.loop(1, n_tm)
-        def _(d):
-            pltpu.make_async_remote_copy(
-                src_ref=tm_send.at[which], dst_ref=tm_in.at[which, d - 1],
-                send_sem=sum_send_sem.at[2 + which], recv_sem=sum_recv_sem.at[2 + which],
-                device_id=tm_peer(d), device_id_type=MESH,
-            ).start()
-
     def all_tm(which):
-        pltpu.make_async_copy(tm_in.at[which], tm_in.at[which], sum_recv_sem.at[2 + which]).wait()
+        wait_sums(TM, which)
         prior = jnp.zeros((1, 128), F32)
         for d in range(1, n_tm):
             prior = prior + jnp.where(tm >= d, tm_in[which, d - 1], 0.0)
         return prior + tm_send[which] + pltpu.roll(prior, 4, 1)
 
     def sums_sent(which):
-        pltpu.make_async_copy(plane_in.at[which], plane_in.at[which], sum_send_sem.at[which]).wait()
-        pltpu.make_async_copy(tm_in.at[which], tm_in.at[which], sum_send_sem.at[2 + which]).wait()
+        for stage in (TM, COL, ROW):
+            arrived = exchanges[stage][3].at[which]
+            pltpu.make_async_copy(arrived, arrived, sum_send_sem.at[2 * stage + which]).wait()
 
     def columns(x, out):
         for side, lo, at in ((0, cols - 8, 7), (1, 0, 0)):
@@ -266,9 +265,9 @@
     none = jnp.zeros((8, xl.shape[-1]), F32)
     s, q = lax.fori_loop(2, frames + 2, add_frame, (none, none))
     moments = pack_moments(jnp.sum(s, axis=0, keepdims=True), jnp.sum(q, axis=0, keepdims=True))
-    pl.semaphore_wait(barrier, plane - 1 + n_tm - 1)
-
-    send_tm(0, moments)
+    pl.semaphore_wait(barrier, n_tm + n_col + n_row - 3)
+
+    send_sums(TM, 0, moments)
     by_row = halo_rows(xl, 0, 2, frames + 2)
     onward = onward_frames(xl, 2, 0, 2)
     for copy in by_row:
@@ -276,13 +275,14 @@
     columns(xl, send_l)
     by_col = halo_columns(send_l, coll, 3)
     onward += onward_rows(xl, 5)
-    send_plane(0, all_tm(0))
+    send_sums(COL, 0, all_tm(0))
     for copy in by_col:
         copy.wait_recv()
     onward += onward_columns(coll, 7)
     for load in loads[1:5]:
         load.wait()
-    all_plane(0, terms1)
+    send_sums(ROW, 0, all_along(COL, 0))
+    all_terms(0, terms1)
 
     build(xl, coll, act, edge, terms1, 2, frames + 2, 0, marks)
     loads[5].wait()
@@ -302,7 +302,7 @@
     build(xl, coll, act, edge, terms1, 0, 2, 1, marks)
     s, q = lax.fori_loop(0, frames - 2, hidden_frame, sums)
     moments = pack_moments(jnp.sum(s, axis=0, keepdims=True), jnp.sum(q, axis=0, keepdims=True))
-    send_tm(1, moments)
+    send_sums(TM, 1, moments)
     onward2 += onward_frames(xh, 20, 1, 2)
     by_row2 += halo_rows(xh, 12, 2, frames)
     for copy in by_row2:
@@ -310,11 +310,12 @@
     columns(xh, send_h)
     by_col2 = halo_columns(send_h, colh, 14)
     onward2 += onward_rows(xh, 16)
-    send_plane(1, all_tm(1))
+    send_sums(COL, 1, all_tm(1))
     for copy in by_col2:
         copy.wait_recv()
     onward2 += onward_columns(colh, 18)
-    all_plane(1, terms2)
+    send_sums(ROW, 1, all_along(COL, 1))
+    all_terms(1, terms2)
     loads[6].wait()
     for copy in onward2:
         copy.wait_recv()
@@ -362,7 +363,6 @@
 def on_device(sizes, latent, gain_first, bias_first, kernel_first, gain_second, bias_second, kernel_second, conv_bias):
     n_tm, n_row, n_col = sizes
     frames, rows, cols, channels = latent.shape
-    plane = n_row * n_col
     per_span = float(frames * rows * n_row * cols * n_col * (channels // GROUPS))
     tile = (frames + 2, rows + 2, cols, channels)
     tall = -(-(rows + 2) // 8) * 8
@@ -394,14 +394,16 @@
             pltpu.VMEM((4, 1, channels), F32),
             pltpu.VMEM((8, channels), F32),
             pltpu.VMEM((2, 1, 128), F32),
-            pltpu.VMEM((2, plane - 1, 1, 128), F32),
+            pltpu.VMEM((2, n_tm - 1, 1, 128), F32),
             pltpu.VMEM((2, 1, 128), F32),
-            pltpu.VMEM((2, n_tm - 1, 1, 128), F32),
+            pltpu.VMEM((2, n_col - 1, 1, 128), F32),
+            pltpu.VMEM((2, 1, 128), F32),
+            pltpu.VMEM((2, n_row - 1, 1, 128), F32),
             pltpu.SemaphoreType.DMA((7,)),
             pltpu.SemaphoreType.DMA((N_COPIES,)),
             pltpu.SemaphoreType.DMA((N_COPIES,)),
-            pltpu.SemaphoreType.DMA((4,)),
-            pltpu.SemaphoreType.DMA((4,)),
+            pltpu.SemaphoreType.DMA((6,)),
+            pltpu.SemaphoreType.DMA((6,)),
         ],
         compiler_params=pltpu.CompilerParams(
             collective_id=0, has_side_effects=True, vmem_limit_bytes=24 * 2**20

time: 49.1 us -> 51.2 us (1.043)
  Pallas kernels: 49 us -> 51.1 us
    pallas_call x1, Pallas kernels: 40.6 us -> 42.7 us  [on_device(): pl.pallas_call(functools.partial(first_kernel, sizes, per_span), out_shap...]
where the time goes in v4:
time: 51.2 us; the launch traced here: 51.1 us
  Pallas kernels  51.1 us (100%)
    pallas_call x1, Pallas kernels, on_device(): pl.pallas_call(functools.partial(first_kernel, sizes, per_span), out_shap...  42.7 us
    pallas_call x1, Pallas kernels, on_device(): pl.pallas_call(functools.partial(second_kernel, sizes), out_shape=jax.Sha...  8.39 us

profile of v4, /device:TPU:1, one launch (start us, length us, event | category | flops | bytes accessed | tf_op | source)
XLA Modules:
  0.0 51.1 jit_solution(5648825189375654274)
XLA Ops:
  0.0 0.0 copy-start
  0.0 42.7 %first_conv.1 = (bf16[6,18,24,256]{3,2,1,0:T(8,128)(2,1)S(1)}, bf16[6,18,24,256]{3,2,1,0:T(8,128)(2,1)S(1)}, bf16[2,6,24,256]{3,2,1,0:T(8,128)(2,1)S(1)}, bf16[27,256,256]{2,1,0:T(8,128)(2,1)S(1)}, f32[8,256]{1,0:T(8,128)S(1)}) custom-call(bf16[4,16,24,256]{3,2,1,0:T(8,128)(2,1)} %lat_hbm.1, bf16[27,256,256]{2,1,0:T(8,128)(2,1)} %bitcast.9, ...), custom_call_target="tpu_custom_call" | custom-call | tf_op jit(solution)/shard_map/first_conv/pallas_call | solution.py:381
  42.7 0.0 copy-done
  42.8 8.4 %second_conv.1 = bf16[4,16,2,48,256]{4,3,2,1,0:T(8,128)(2,1)} custom-call(bf16[6,18,24,256]{3,2,1,0:T(8,128)(2,1)S(1)} %get-tuple-element.10.xl, bf16[6,18,24,256]{3,2,1,0:T(8,128)(2,1)S(1)} %get-tuple-element.11.xh, bf16[2,6,24,256]{3,2,1,0:T(8,128)(2,1)S(1)} %get-tuple-element.12.colh, bf16[27,256,256]{2,1,0:T(8,128)(2,1)S(1)} %get-tuple-element.13.w2, ...), custom_call_target="tpu_custom_call" | custom-call | tf_op jit(solution)/shard_map/second_conv/pallas_call | solution.py:426
Async XLA Ops:
  0.0 42.7 %copy-start = (f32[256]{0:T(256)S(1)}, f32[256]{0:T(256)}, u32[]{:S(2)}) copy-start(f32[256]{0:T(256)} %param.15) | copy-start | bytes 3076

commit v5 on v3

--- a/solution.py
+++ b/solution.py
@@ -125,7 +125,6 @@
     tm, row, col = lax.axis_index("tm"), lax.axis_index("row"), lax.axis_index("col")
     frames, rows, cols = xl.shape[0] - 2, xl.shape[1] - 2, xl.shape[2]
     plane = n_row * n_col
-    mine = row * n_col + col
     marks = marks_of(n_row, n_col)
 
     loads = [
@@ -141,8 +140,11 @@
         load.start()
 
     def plane_peer(d):
-        at = lax.rem(mine + d, plane)
-        return (tm, at // n_col, lax.rem(at, n_col))
+        return (tm, lax.rem(row + d // n_col, n_row), lax.rem(col + d % n_col, n_col))
+
+    def plane_hops(d):
+        down, along = d // n_col, d % n_col
+        return min(down, n_row - down) + min(along, n_col - along)
 
     def tm_peer(d):
         return (lax.rem(tm + d, n_tm), row, col)
@@ -175,8 +177,7 @@
     def send_plane(which, moments):
         sum_send[which] = moments
 
-        @pl.loop(1, plane)
-        def _(d):
+        for d in sorted(range(1, plane), key=plane_hops, reverse=True):
             pltpu.make_async_remote_copy(
                 src_ref=sum_send.at[which], dst_ref=plane_in.at[which, d - 1],
                 send_sem=sum_send_sem.at[which], recv_sem=sum_recv_sem.at[which],
@@ -200,8 +201,7 @@
     def send_tm(which, moments):
         tm_send[which] = moments
 
-        @pl.loop(1, n_tm)
-        def _(d):
+        for d in sorted(range(1, n_tm), key=lambda d: min(d, n_tm - d), reverse=True):
             pltpu.make_async_remote_copy(
                 src_ref=tm_send.at[which], dst_ref=tm_in.at[which, d - 1],
                 send_sem=sum_send_sem.at[2 + which], recv_sem=sum_recv_sem.at[2 + which],

time: 49.1 us -> 49.1 us (level)
  no operation moved by 1% of the time
where the time goes in v5:
time: 49.1 us; the launch traced here: 49 us
  Pallas kernels  49 us (100%)
    pallas_call x1, Pallas kernels, on_device(): pl.pallas_call(functools.partial(first_kernel, sizes, per_span), out_shap...  40.6 us
    pallas_call x1, Pallas kernels, on_device(): pl.pallas_call(functools.partial(second_kernel, sizes), out_shape=jax.Sha...  8.39 us

profile of v5, /device:TPU:1, one launch (start us, length us, event | category | flops | bytes accessed | tf_op | source)
XLA Modules:
  0.0 49.0 jit_solution(9250019419104038478)
XLA Ops:
  0.0 0.0 copy-start
  0.0 40.6 %first_conv.1 = (bf16[6,18,24,256]{3,2,1,0:T(8,128)(2,1)S(1)}, bf16[6,18,24,256]{3,2,1,0:T(8,128)(2,1)S(1)}, bf16[2,6,24,256]{3,2,1,0:T(8,128)(2,1)S(1)}, bf16[27,256,256]{2,1,0:T(8,128)(2,1)S(1)}, f32[8,256]{1,0:T(8,128)S(1)}) custom-call(bf16[4,16,24,256]{3,2,1,0:T(8,128)(2,1)} %lat_hbm.1, bf16[27,256,256]{2,1,0:T(8,128)(2,1)} %bitcast.9, ...), custom_call_target="tpu_custom_call" | custom-call | tf_op jit(solution)/shard_map/first_conv/pallas_call | solution.py:381
  40.6 0.0 copy-done
  40.6 8.4 %second_conv.1 = bf16[4,16,2,48,256]{4,3,2,1,0:T(8,128)(2,1)} custom-call(bf16[6,18,24,256]{3,2,1,0:T(8,128)(2,1)S(1)} %get-tuple-element.10.xl, bf16[6,18,24,256]{3,2,1,0:T(8,128)(2,1)S(1)} %get-tuple-element.11.xh, bf16[2,6,24,256]{3,2,1,0:T(8,128)(2,1)S(1)} %get-tuple-element.12.colh, bf16[27,256,256]{2,1,0:T(8,128)(2,1)S(1)} %get-tuple-element.13.w2, ...), custom_call_target="tpu_custom_call" | custom-call | tf_op jit(solution)/shard_map/second_conv/pallas_call | solution.py:424
Async XLA Ops:
  0.0 40.6 %copy-start = (f32[256]{0:T(256)S(1)}, f32[256]{0:T(256)}, u32[]{:S(2)}) copy-start(f32[256]{0:T(256)} %param.15) | copy-start | bytes 3076
